TPU v7x, 32 devices: a whole 2x2x4 slice. The times are simulated.
32 devices in a mesh: group: 2 (over y), seq: 4 (over z), req: 2 (over x), sub: 2 (over core).
Axes of the slice: x: 2, y: 2, z: 4, core: 2. Of those that a mesh axis runs over, the one named last changes fastest.
Arguments:
- latent_codes: bfloat16 [2, 16, 2048, 512], P(None, ('group', 'req', 'sub'), 'seq'), parts along dimension 1, may hold values from -6 to 6
- latent_scales: bfloat16 [2, 16, 2048, 4], P(None, ('group', 'req', 'sub'), 'seq'), parts along dimension 1, may hold values from 0.34 to 3.5
- rope_keys: bfloat16 [2, 16, 2048, 64], P(None, ('group', 'req', 'sub'), 'seq'), parts along dimension 1, may hold values from -6 to 6
- lengths: int32 [16], P(('group', 'req', 'sub')), parts along dimension 0, may hold values from 256 to 2048, as said below
- query_latent: bfloat16 [2, 16, 4, 128, 512], P(None, ('group', 'req', 'sub'), None, 'seq'), parts along dimension 1, may hold values from -64 to 64
- query_rope: bfloat16 [2, 16, 4, 128, 64], P(None, ('group', 'req', 'sub'), None, 'seq'), parts along dimension 1, may hold values from -8 to 8
- new_latent: bfloat16 [2, 16, 4, 512], P(None, ('group', 'req', 'sub')), parts along dimension 1, may hold values from -9 to 9
- new_rope: bfloat16 [2, 16, 4, 64], P(None, ('group', 'req', 'sub')), parts along dimension 1, may hold values from -6 to 6
Outputs:
- attended: bfloat16 [2, 16, 4, 128, 512], P(None, ('group', 'req', 'sub'), None, 'seq'), parts along dimension 1
- cache_codes: bfloat16 [2, 16, 512, 4, 512], P(None, ('group', 'req', 'sub'), None, 'seq'), parts along dimension 1
- cache_scales: bfloat16 [2, 16, 512, 4, 4], P(None, ('group', 'req', 'sub'), None, 'seq'), parts along dimension 1
- cache_rope: bfloat16 [2, 16, 512, 4, 64], P(None, ('group', 'req', 'sub'), None, 'seq'), parts along dimension 1
There are 2 independent parts, one for each index of `group`. A program takes and returns all parts, laid end to end along the dimension named above; each array names one. Nothing has to cross between parts.
Inputs may be any that keep to these rules, and one draw needn't show every extreme that they name: `lengths`: one request is exactly 2048 long.
All inputs are finite; a program needn't handle non-finite values.
Results may differ from a plain program's by a relative error of at most 0.013.
Values may be sent and summed in bfloat16 or wider, within the bound.
A program may use at most 64 MiB of HBM per device.

v0:
```python
import jax
import jax.numpy as jnp
from jax import lax
from jax.sharding import PartitionSpec as P

softmax_gain = 192.0 ** (-0.5)
masked_score = -1e30


def dequantize(code_values, scale_values):
    blocks = scale_values.shape[-1]
    latent_width = code_values.shape[-1]
    shaped = code_values.astype(jnp.float32).reshape(
        code_values.shape[:-1] + (blocks, latent_width // blocks)
    )
    scaled = shaped * scale_values.astype(jnp.float32)[..., None]
    return scaled.reshape(code_values.shape).astype(jnp.bfloat16)


def shard_partial(
    lat_query, rope_query, key_rows, rope_rows, usable, new_keys, new_rope_rows, holds_new
):
    tokens_new, head_count, latent_width = lat_query.shape
    query_rows = lat_query.reshape(tokens_new * head_count, latent_width)
    query_pos = rope_query.reshape(tokens_new * head_count, rope_query.shape[-1])
    scores = jnp.dot(query_rows, key_rows.T, preferred_element_type=jnp.float32)
    scores = (
        scores + jnp.dot(query_pos, rope_rows.T, preferred_element_type=jnp.float32)
    ) * softmax_gain
    fresh_scores = jnp.dot(query_rows, new_keys.T, preferred_element_type=jnp.float32)
    fresh_scores = (
        fresh_scores + jnp.dot(query_pos, new_rope_rows.T, preferred_element_type=jnp.float32)
    ) * softmax_gain
    token_of_row = jnp.arange(tokens_new * head_count, dtype=jnp.int32) // head_count
    causal = (jnp.arange(tokens_new, dtype=jnp.int32)[None, :] <= token_of_row[:, None]) & holds_new
    scores = jnp.where(usable[None, :], scores, masked_score)
    fresh_scores = jnp.where(causal, fresh_scores, masked_score)
    group_peak = jnp.maximum(jnp.max(scores, 1), jnp.max(fresh_scores, 1)).astype(jnp.bfloat16)
    peak_float = group_peak.astype(jnp.float32)[:, None]
    weights = jnp.where(usable[None, :], jnp.exp(scores - peak_float), 0.0).astype(jnp.bfloat16)
    fresh_weights = jnp.where(causal, jnp.exp(fresh_scores - peak_float), 0.0).astype(jnp.bfloat16)
    group_total = jnp.sum(weights.astype(jnp.float32), 1) + jnp.sum(
        fresh_weights.astype(jnp.float32), 1
    )
    group_sum = jnp.dot(weights, key_rows, preferred_element_type=jnp.float32)
    group_sum = group_sum + jnp.dot(fresh_weights, new_keys, preferred_element_type=jnp.float32)
    return (
        group_sum.astype(jnp.bfloat16).reshape(tokens_new, head_count, latent_width),
        group_peak.reshape(tokens_new, head_count),
        group_total.astype(jnp.bfloat16).reshape(tokens_new, head_count),
    )


def merge_groups(pieces):
    group_sum, group_peak, group_total = pieces
    peak_float = group_peak.astype(jnp.float32)
    overall = jnp.max(peak_float, 0)
    factor = jnp.exp(peak_float - overall)
    numerator = jnp.sum(factor[..., None] * group_sum.astype(jnp.float32), 0)
    denominator = jnp.sum(factor * group_total.astype(jnp.float32), 0)
    return (numerator / denominator[..., None]).astype(jnp.bfloat16)


def per_device(
    latent_codes, latent_scales, rope_keys, lengths, query_latent, query_rope, new_latent, new_rope
):
    shard_count = lax.axis_size("seq")
    seq_index = lax.axis_index("seq")
    layer_count, request_count, span, latent_width = latent_codes.shape
    lat_query, rope_query = (
        lax.all_gather(query_latent, "seq", axis=3, tiled=True),
        lax.all_gather(query_rope, "seq", axis=3, tiled=True),
    )

    def regroup_rows(values):
        return values.reshape(
            values.shape[0], values.shape[1], span // shard_count, shard_count, values.shape[-1]
        )

    codes_moved, scales_moved, rope_moved = (
        lax.all_to_all(regroup_rows(latent_codes), "seq", split_axis=3, concat_axis=2, tiled=True),
        lax.all_to_all(regroup_rows(latent_scales), "seq", split_axis=3, concat_axis=2, tiled=True),
        lax.all_to_all(regroup_rows(rope_keys), "seq", split_axis=3, concat_axis=2, tiled=True),
    )
    offsets = jnp.arange(span, dtype=jnp.int32)
    key_rows = dequantize(latent_codes, latent_scales)
    positions = seq_index * span + offsets
    usable = positions[None, :] < lengths[:, None]
    holds_new = seq_index == 0
    per_request = jax.vmap(shard_partial, in_axes=(0, 0, 0, 0, 0, 0, 0, None))
    per_layer = jax.vmap(per_request, in_axes=(0, 0, 0, 0, None, 0, 0, None))
    group_sum, group_peak, group_total = per_layer(
        lat_query, rope_query, key_rows, rope_keys, usable, new_latent, new_rope, holds_new
    )
    attended = merge_groups(
        (
            lax.all_to_all(group_sum[None], "seq", split_axis=4, concat_axis=0, tiled=True),
            lax.all_to_all(group_peak[None], "seq", split_axis=4, concat_axis=0, tiled=True),
            lax.all_to_all(group_total[None], "seq", split_axis=4, concat_axis=0, tiled=True),
        )
    )
    return (attended, codes_moved, scales_moved, rope_moved)


def solution(mesh):
    placed = (
        P(None, ("group", "req", "sub"), "seq", None),
        P(None, ("group", "req", "sub"), "seq", None),
        P(None, ("group", "req", "sub"), "seq", None),
        P(("group", "req", "sub")),
        P(None, ("group", "req", "sub"), None, "seq", None),
        P(None, ("group", "req", "sub"), None, "seq", None),
        P(None, ("group", "req", "sub"), None, None),
        P(None, ("group", "req", "sub"), None, None),
    )
    return jax.shard_map(
        per_device,
        mesh=mesh,
        in_specs=placed,
        out_specs=(
            P(None, ("group", "req", "sub"), None, "seq", None),
            P(None, ("group", "req", "sub"), None, "seq", None),
            P(None, ("group", "req", "sub"), None, "seq", None),
            P(None, ("group", "req", "sub"), None, "seq", None),
        ),
        check_vma=False,
    )
```

profile of v0, /device:TPU:0, one launch (start us, length us, event | category | flops | bytes accessed | tf_op | source)
XLA Modules:
  0.0 215.6 jit_solution(11127280630018597931)
XLA Ops:
  7.2 0.0 copy-start
  7.2 0.0 all-gather.2.cloned.1.call-start
  7.2 0.7 all-gather.2.cloned.1.call-update
  7.9 1.8 reshape.126
  9.8 0.8 copy.66
  10.6 6.3 %all-to-all-start.4 = ((bf16[2,2,128,4,4]{2,4,1,0,3:T(4,128)(2,1)}), bf16[2,2,128,4,4]{2,4,1,0,3:T(4,128)(2,1)S(1)}, u32[]{:S(2)}, u32[]{:S(2)}) async-start(bf16[2,2,128,4,4]{2,4,1,0,3:T(4,128)(2,1)} %copy.66), calls=%async_computation.4 | async-start | bytes 32768 | tf_op jit(solution)/shard_map/all_to_all | solution.py:82
  16.9 1.2 copy.68
  18.1 1.0 copy.69
  19.2 3.4 %all-to-all-done.4 = bf16[2,2,128,4,4]{2,4,1,0,3:T(4,128)(2,1)S(1)} async-done(((bf16[2,2,128,4,4]{2,4,1,0,3:T(4,128)(2,1)}), bf16[2,2,128,4,4]{2,4,1,0,3:T(4,128)(2,1)S(1)}, u32[]{:S(2)}, u32[]{:S(2)}) %all-to-all-start.4) | async-done | bytes 16416 | tf_op jit(solution)/shard_map/all_to_all | solution.py:82
  22.5 3.4 %all-to-all-start.5 = ((bf16[2,2,128,4,64]{2,4,1,0,3:T(8,128)(2,1)}), bf16[2,2,128,4,64]{2,4,1,0,3:T(8,128)(2,1)S(1)}, u32[]{:S(2)}, u32[]{:S(2)}) async-start(bf16[2,2,128,4,64]{2,4,1,0,3:T(8,128)(2,1)} %copy.69), calls=%async_computation.5 | async-start | bytes 524288 | tf_op jit(solution)/shard_map/all_to_all | solution.py:83
  25.9 1.0 copy.57
  26.9 3.9 %mul.38 = f32[2,2,512,4,128]{4,3,2,1,0:T(4,128)} broadcast(f32[2,2,512,4]{3,2,1,0:T(8,128)S(1)} %copy.57), dimensions={0,1,2,3} | broadcast | bytes 4227072 | tf_op jit(solution)/shard_map/mul | solution.py:16
  30.8 0.0 copy-start.2
  30.8 5.6 %mul.39 = f32[2,2,512,512]{3,2,1,0:T(8,128)} reshape(f32[2,2,512,4,128]{4,3,2,1,0:T(4,128)} %mul.38) | data formatting | bytes 8388608 | tf_op jit(solution)/shard_map/mul | solution.py:16
  36.4 0.0 copy-done.2
  36.4 2.2 %copy.63 = bf16[2,2,512,512]{3,1,2,0:T(2,128)(2,1)S(1)} copy(bf16[2,2,512,512]{3,2,1,0:T(8,128)(2,1)S(1)} %copy-done.2) | data formatting | bytes 4194304 | tf_op args[0]
  38.6 0.0 copy-start.4
  38.6 0.0 copy-start.6
  38.6 0.0 copy-start.5
  38.6 0.0 copy-start.3
  38.6 2.0 copy.64
  40.6 1.7 all-to-all-done.5
  42.3 4.5 %all-to-all-start.3 = ((bf16[2,2,128,4,512]{4,2,1,0,3:T(8,128)(2,1)}), bf16[2,2,128,4,512]{4,2,1,0,3:T(8,128)(2,1)}, u32[]{:S(2)}, u32[]{:S(2)}) async-start(bf16[2,2,128,4,512]{4,2,1,0,3:T(8,128)(2,1)} %copy.64), calls=%async_computation.3 | async-start | bytes 4194304 | tf_op jit(solution)/shard_map/all_to_all | solution.py:81
  46.8 0.0 copy-done.4
  46.8 71.2 %all_gather.7 = bf16[2,2,4,128,64]{4,3,2,1,0:T(8,128)(2,1)S(1)} all-gather(bf16[2,2,4,32,64]{4,3,2,1,0:T(8,128)(2,1)S(1)} %copy-done.4), channel_id=1, replica_groups=mesh['group'=2,'seq'=4,'req'=2,'sub'=2] {'seq'}, dimensions={3}, use_global_device_ids=true | all-gather | bytes 327680 | tf_op jit(solution)/shard_map/all_gather | solution.py:72
  118.0 0.0 copy-done.6
  118.0 0.1 broadcast_compare_fusion
  118.1 0.0 copy-done.5
  118.1 0.2 fusion.17
  118.3 0.0 copy-done.3
  118.3 2.8 %fusion.16 = f32[2,2,512,512]{2,3,1,0:T(8,128)} fusion(bf16[2,2,512,64]{3,2,1,0:T(8,128)(2,1)S(1)} %bitcast.77, bf16[2,2,512,64]{2,3,1,0:T(8,128)(2,1)S(1)} %copy-done.3), kind=kOutput, calls=%fused_computation.39 | convolution fusion | flops 134217728 | bytes 4718592 | tf_op jit(solution)/shard_map/vmap(vmap())/dot_general | solution.py:28
  121.1 0.0 all-gather.2.cloned.1.call-done
  121.1 0.0 copy-done
  121.1 2.3 %fusion.15 = (bf16[2,2,512]{2,1,0:T(2,128)(2,1)S(1)}, f32[2,2,512,4]{2,3,1,0:T(4,128)S(1)}) fusion(f32[2,2,512,4]{2,3,1,0:T(4,128)S(1)} %fusion.17, bf16[2,2,512,512]{3,2,1,0:T(8,128)(2,1)} %bitcast.74, bf16[2,2,4,512]{3,2,1,0:T(4,128)(2,1)S(1)} %copy-done, pred[512,4]{0,1:T(4,128)(4,1)S(1)} %fusion.8), kind=kOutput, calls=%fused_computation.38 | convolution fusion | flops 8419328 | bytes 2185216 | tf_op jit(solution)/shard_map/vmap(vmap())/dot_general | solution.py:30
  123.4 5.6 %fusion.14 = (bf16[2,2,512]{2,1,0:T(2,128)(2,1)S(1)}, f32[2,2,512,512]{2,3,1,0:T(8,128)S(1)}) fusion(f32[2,2,512,512]{2,3,1,0:T(8,128)} %fusion.16, bf16[2,2,512,512]{3,2,1,0:T(8,128)(2,1)} %bitcast.75, f32[2,2,512,512]{3,2,1,0:T(8,128)} %mul.39, bf16[2,2,512,512]{3,2,1,0:T(8,128)(2,1)S(1)} %copy-done.2, pred[2,512]{1,0:T(4,128)(4,1)S(1)} %broadcast_compare_fusion), kind=kOutput, calls=%fused_computation.37 | convolution fusion | flops 1081079808 | bytes 16782336 | tf_op jit(solution)/shard_map/vmap(vmap())/dot_general | solution.py:26
  128.9 0.0 copy-start.1
  129.0 1.9 copy-done.1
  130.9 0.7 convert_reduce_fusion
  131.7 0.2 copy.62
  131.9 0.8 reshape.135
  132.7 0.0 all-to-all-done.3
  132.7 5.0 %all-to-all-start.2 = ((bf16[4,2,256]{2,1,0:T(2,128)(2,1)}), bf16[4,2,256]{2,1,0:T(2,128)(2,1)S(1)}, u32[]{:S(2)}, u32[]{:S(2)}) async-start(bf16[4,2,256]{2,1,0:T(2,128)(2,1)} %reshape.135), calls=%async_computation.2 | async-start | bytes 8192 | tf_op jit(solution)/shard_map/all_to_all | solution.py:99
  137.6 7.1 %fusion.5 = f32[2,2,512,512]{3,2,1,0:T(8,128)} fusion(f32[2,2,512,512]{2,3,1,0:T(8,128)} %copy-done.1, f32[2,2,512]{2,1,0:T(2,128)S(1)} %get-tuple-element.20, pred[2,512]{1,0:T(4,128)(4,1)S(1)} %broadcast_compare_fusion, f32[2,2,512,512]{3,2,1,0:T(8,128)} %mul.39, bf16[2,2,512,512]{3,2,1,0:T(8,128)(2,1)S(1)} %copy-done.2), kind=kOutput, calls=%fused_computation.13 | convolution fusion | flops 1080033280 | bytes 14689280 | tf_op jit(solution)/shard_map/vmap(vmap())/dot_general | solution.py:45
  144.8 0.2 copy.59
  145.0 0.8 reshape.133
  145.7 0.0 all-to-all-done.2
  145.7 5.1 %all-to-all-start = ((bf16[4,2,256]{2,1,0:T(2,128)(2,1)}), bf16[4,2,256]{2,1,0:T(2,128)(2,1)S(1)}, u32[]{:S(2)}, u32[]{:S(2)}) async-start(bf16[4,2,256]{2,1,0:T(2,128)(2,1)} %reshape.133), calls=%async_computation | async-start | bytes 8192 | tf_op jit(solution)/shard_map/all_to_all | solution.py:98
  150.8 3.0 %add_convert_fusion = bf16[2,2,512,512]{3,2,1,0:T(8,128)(2,1)S(1)} fusion(f32[2,2,512,512]{3,2,1,0:T(8,128)} %fusion.5, bf16[2,2,4,512]{3,2,1,0:T(4,128)(2,1)S(1)} %copy-done, f32[2,2,512,4]{2,3,1,0:T(4,128)S(1)} %get-tuple-element.27, f32[2,2,512]{2,1,0:T(2,128)S(1)} %get-tuple-element.20, pred[512,4]{0,1:T(4,128)(4,1)S(1)} %fusion.8), kind=kOutput, calls=%fused_computation.6 | convolution fusion | flops 10510336 | bytes 6350848 | tf_op jit(solution)/shard_map/vmap(vmap())/dot_general | solution.py:46
  153.8 3.0 %copy.61 = bf16[1,2,2,4,128,512]{5,3,2,1,0,4:T(4,128)(2,1)} copy(bf16[1,2,2,4,128,512]{5,4,3,2,1,0:T(8,128)(2,1)S(1)} %bitcast.72) | data formatting | bytes 4194304 | tf_op jit(solution)/shard_map/broadcast_in_dim;vmap(vmap())/reshape | solution.py:97
  156.8 0.0 all-to-all-done
  156.8 5.1 %all-to-all-start.1 = ((bf16[1,2,2,4,128,512]{5,3,2,1,0,4:T(4,128)(2,1)}), bf16[1,2,2,4,128,512]{5,3,2,1,0,4:T(4,128)(2,1)S(1)}, u32[]{:S(2)}, u32[]{:S(2)}) async-start(bf16[1,2,2,4,128,512]{5,3,2,1,0,4:T(4,128)(2,1)} %copy.61), calls=%async_computation.1 | async-start | bytes 4194304 | tf_op jit(solution)/shard_map/all_to_all | solution.py:97
  161.9 0.6 copy_bitcast_fusion
  162.5 0.7 bitcast_bitcast_fusion
  163.2 3.1 %copy.65 = bf16[2,2,128,4,512]{4,2,3,1,0:T(8,128)(2,1)} copy(bf16[2,2,128,4,512]{4,2,1,0,3:T(8,128)(2,1)} %all-to-all-done.3) | data formatting | bytes 4194304 | tf_op jit(solution)/shard_map/all_to_all | solution.py:81
  166.3 0.3 reshape.134
  166.6 0.2 reduce_max.34
  166.8 0.3 reshape.136
  167.1 0.3 fusion.6
  167.4 38.4 %all-to-all-done.1 = bf16[1,2,2,4,128,512]{5,3,2,1,0,4:T(4,128)(2,1)S(1)} async-done(((bf16[1,2,2,4,128,512]{5,3,2,1,0,4:T(4,128)(2,1)}), bf16[1,2,2,4,128,512]{5,3,2,1,0,4:T(4,128)(2,1)S(1)}, u32[]{:S(2)}, u32[]{:S(2)}) %all-to-all-start.1) | async-done | bytes 2097184 | tf_op jit(solution)/shard_map/all_to_all | solution.py:97
  205.9 1.5 fusion
  207.4 0.3 divide_convert_fusion
  207.7 1.1 copy.71
  (9 shorter events, 0.1 us)
Async XLA Ops:
  7.2 113.9 %copy-start = (bf16[2,2,4,512]{3,2,1,0:T(4,128)(2,1)S(1)}, bf16[2,2,4,512]{3,2,1,0:T(4,128)(2,1)}, u32[]{:S(2)}) copy-start(bf16[2,2,4,512]{3,2,1,0:T(4,128)(2,1)} %param.14) | copy-start | bytes 49156
  7.2 113.9 %all-gather.2.cloned.1.call-start = ((), (), s32[]{:S(2)}) async-start(), calls=%async_computation.6 | async-start | bytes 2621440 | tf_op jit(solution)/shard_map/all_gather | solution.py:71
  10.6 11.9 %all-to-all-start.4 = ((bf16[2,2,128,4,4]{2,4,1,0,3:T(4,128)(2,1)}), bf16[2,2,128,4,4]{2,4,1,0,3:T(4,128)(2,1)S(1)}, u32[]{:S(2)}, u32[]{:S(2)}) async-start(bf16[2,2,128,4,4]{2,4,1,0,3:T(4,128)(2,1)} %copy.66), calls=%async_computation.4 | async-start | bytes 32768 | tf_op jit(solution)/shard_map/all_to_all | solution.py:82
  22.5 19.8 %all-to-all-start.5 = ((bf16[2,2,128,4,64]{2,4,1,0,3:T(8,128)(2,1)}), bf16[2,2,128,4,64]{2,4,1,0,3:T(8,128)(2,1)S(1)}, u32[]{:S(2)}, u32[]{:S(2)}) async-start(bf16[2,2,128,4,64]{2,4,1,0,3:T(8,128)(2,1)} %copy.69), calls=%async_computation.5 | async-start | bytes 524288 | tf_op jit(solution)/shard_map/all_to_all | solution.py:83
  30.8 5.6 %copy-start.2 = (bf16[2,2,512,512]{3,2,1,0:T(8,128)(2,1)S(1)}, bf16[2,2,512,512]{3,2,1,0:T(8,128)(2,1)}, u32[]{:S(2)}) copy-start(bf16[2,2,512,512]{3,2,1,0:T(8,128)(2,1)} %param.8) | copy-start | bytes 6291460
  38.6 8.2 %copy-start.4 = (bf16[2,2,4,32,64]{4,3,2,1,0:T(8,128)(2,1)S(1)}, bf16[2,2,4,32,64]{4,3,2,1,0:T(8,128)(2,1)}, u32[]{:S(2)}) copy-start(bf16[2,2,4,32,64]{4,3,2,1,0:T(8,128)(2,1)} %param.13) | copy-start | bytes 196612
  38.6 79.4 %copy-start.6 = (s32[2]{0:T(128)S(1)}, s32[2]{0:T(128)}, u32[]{:S(2)}) copy-start(s32[2]{0:T(128)} %param.11) | copy-start | bytes 28
  38.6 79.5 %copy-start.5 = (bf16[2,2,4,64]{3,2,1,0:T(4,128)(2,1)S(1)}, bf16[2,2,4,64]{3,2,1,0:T(4,128)(2,1)}, u32[]{:S(2)}) copy-start(bf16[2,2,4,64]{3,2,1,0:T(4,128)(2,1)} %param.15) | copy-start | bytes 6148
  38.6 79.7 %copy-start.3 = (bf16[2,2,512,64]{2,3,1,0:T(8,128)(2,1)S(1)}, bf16[2,2,512,64]{2,3,1,0:T(8,128)(2,1)}, u32[]{:S(2)}) copy-start(bf16[2,2,512,64]{2,3,1,0:T(8,128)(2,1)} %param.10) | copy-start | bytes 786436
  42.3 90.3 %all-to-all-start.3 = ((bf16[2,2,128,4,512]{4,2,1,0,3:T(8,128)(2,1)}), bf16[2,2,128,4,512]{4,2,1,0,3:T(8,128)(2,1)}, u32[]{:S(2)}, u32[]{:S(2)}) async-start(bf16[2,2,128,4,512]{4,2,1,0,3:T(8,128)(2,1)} %copy.64), calls=%async_computation.3 | async-start | bytes 4194304 | tf_op jit(solution)/shard_map/all_to_all | solution.py:81
  128.9 2.0 copy-start.1
  132.7 13.1 %all-to-all-start.2 = ((bf16[4,2,256]{2,1,0:T(2,128)(2,1)}), bf16[4,2,256]{2,1,0:T(2,128)(2,1)S(1)}, u32[]{:S(2)}, u32[]{:S(2)}) async-start(bf16[4,2,256]{2,1,0:T(2,128)(2,1)} %reshape.135), calls=%async_computation.2 | async-start | bytes 8192 | tf_op jit(solution)/shard_map/all_to_all | solution.py:99
  145.7 11.0 %all-to-all-start = ((bf16[4,2,256]{2,1,0:T(2,128)(2,1)}), bf16[4,2,256]{2,1,0:T(2,128)(2,1)S(1)}, u32[]{:S(2)}, u32[]{:S(2)}) async-start(bf16[4,2,256]{2,1,0:T(2,128)(2,1)} %reshape.133), calls=%async_computation | async-start | bytes 8192 | tf_op jit(solution)/shard_map/all_to_all | solution.py:98
  156.8 49.1 %all-to-all-start.1 = ((bf16[1,2,2,4,128,512]{5,3,2,1,0,4:T(4,128)(2,1)}), bf16[1,2,2,4,128,512]{5,3,2,1,0,4:T(4,128)(2,1)S(1)}, u32[]{:S(2)}, u32[]{:S(2)}) async-start(bf16[1,2,2,4,128,512]{5,3,2,1,0,4:T(4,128)(2,1)} %copy.61), calls=%async_computation.1 | async-start | bytes 4194304 | tf_op jit(solution)/shard_map/all_to_all | solution.py:97
Sparse Core Ops, SparseCore 0:
  9.6 73.4 all-gather.1
where the time goes:
time: 216 us
  blocking collectives  71.2 us (33%)
  waiting for transfers between devices  44.2 us (20%)
  local copies, waits for them, and re-layouts  32.4 us (15%)
  starting transfers between devices  29.4 us (14%)
  matrix products  20.9 us (10%)
  between operations  14.3 us (7%)
  other arithmetic  3.24 us (2%)
    all_gather x1, blocking collectives, per_device(): lax.all_gather(query_rope, 'seq', axis=3, tiled=True)  71.2 us
    all_to_all x1, waiting for transfers between devices, per_device(): lax.all_to_all(group_sum[None], 'seq', split_axis=4, concat_axis=0, tiled...  38.4 us
    mul x2, local copies, waits for them, and re-layouts, dequantize(): scaled = shaped * scale_values.astype(jnp.float32)[..., None]  9.47 us
    unnamed x22, local copies, waits for them, and re-layouts  9.29 us
    dot_general x1, matrix products, shard_partial(): group_sum = jnp.dot(weights, key_rows, preferred_element_type=jnp.float32)  7.14 us
    all_to_all x1, starting transfers between devices, per_device(): lax.all_to_all(regroup_rows(latent_scales), 'seq', split_axis=3, concat_a...  6.32 us
    reshape x4, local copies, waits for them, and re-layouts, regroup_rows(): values.reshape(values.shape[0], values.shape[1], span // shard_count, sha...  5.68 us
    dot_general x1, matrix products, shard_partial(): scores = jnp.dot(query_rows, key_rows.T, preferred_element_type=jnp.float32)  5.57 us
  transfers between devices with their start and end apart: 7, of which 3 were waited for; matrix products, arithmetic and copies ran while one was open for 24% of the time, Pallas kernels for 0%

commit v1 on v0

--- a/solution.py
+++ b/solution.py
@@ -95,7 +95,15 @@
     attended = merge_groups(
         (
             lax.all_to_all(group_sum[None], "seq", split_axis=4, concat_axis=0, tiled=True),
-            lax.all_to_all(group_peak[None], "seq", split_axis=4, concat_axis=0, tiled=True),
+            jnp.concatenate(
+                lax.all_to_all(
+                    jnp.stack(jnp.split(group_peak[None], lax.axis_size("seq"), axis=4)),
+                    "seq",
+                    0,
+                    0,
+                ),
+                axis=0,
+            ),
             lax.all_to_all(group_total[None], "seq", split_axis=4, concat_axis=0, tiled=True),
         )
     )

time: 216 us -> 201 us (0.931)
  blocking collectives: 71.2 us -> 31.6 us
  waiting for transfers between devices: 44.2 us -> 70.6 us
  starting transfers between devices: 29.4 us -> 26.4 us
  other arithmetic: 3.24 us -> 5.79 us
    all_gather x1, blocking collectives: 71.2 us -> 31.6 us  [per_device(): lax.all_gather(query_rope, 'seq', axis=3, tiled=True)]
    all_to_all x1, waiting for transfers between devices: 0.01 us -> 22.8 us  [per_device(): lax.all_to_all(regroup_rows(latent_codes), 'seq', split_axis=3, concat_ax...]
    all_to_all x1, waiting for transfers between devices: 0.01 us -> 4.58 us  [per_device(): lax.all_to_all(jnp.stack(jnp.split(group_peak[None], lax.axis_size('seq')...]
    reduce_sum x1, other arithmetic: 0.73 us -> 3.08 us  [shard_partial(): jnp.sum(weights.astype(jnp.float32), 1)]
    unnamed x22 -> x20, local copies, waits for them, and re-layouts: 9.29 us -> 7.4 us
  transfers between devices with their start and end apart: 7 -> 7, of which waited for: 3 -> 4; matrix products, arithmetic and copies ran while one was open for 24% -> 27% of each run, Pallas kernels for 0% -> 0%
where the time goes in v1:
time: 201 us
  waiting for transfers between devices  70.6 us (35%)
  blocking collectives  31.6 us (16%)
  local copies, waits for them, and re-layouts  30.3 us (15%)
  starting transfers between devices  26.4 us (13%)
  matrix products  21.6 us (11%)
  between operations  14.2 us (7%)
  other arithmetic  5.79 us (3%)
    all_to_all x1, waiting for transfers between devices, per_device(): lax.all_to_all(group_sum[None], 'seq', split_axis=4, concat_axis=0, tiled...  39.9 us
    all_gather x1, blocking collectives, per_device(): lax.all_gather(query_rope, 'seq', axis=3, tiled=True)  31.6 us
    all_to_all x1, waiting for transfers between devices, per_device(): lax.all_to_all(regroup_rows(latent_codes), 'seq', split_axis=3, concat_ax...  22.8 us
    mul x2, local copies, waits for them, and re-layouts, dequantize(): scaled = shaped * scale_values.astype(jnp.float32)[..., None]  9.46 us
    dot_general x1, matrix products, shard_partial(): scores = jnp.dot(query_rows, key_rows.T, preferred_element_type=jnp.float32)  7.53 us
    unnamed x20, local copies, waits for them, and re-layouts  7.4 us
    all_to_all x1, starting transfers between devices, per_device(): lax.all_to_all(regroup_rows(latent_scales), 'seq', split_axis=3, concat_a...  6.32 us
    dot_general x1, matrix products, shard_partial(): group_sum = jnp.dot(weights, key_rows, preferred_element_type=jnp.float32)  5.94 us
  transfers between devices with their start and end apart: 7, of which 4 were waited for; matrix products, arithmetic and copies ran while one was open for 27% of the time, Pallas kernels for 0%

profile of v1, /device:TPU:0, one launch (start us, length us, event | category | flops | bytes accessed | tf_op | source)
XLA Modules:
  0.0 200.6 jit_solution(10585755481284556585)
XLA Ops:
  7.2 0.0 copy-start
  7.2 0.0 copy-start.4
  7.2 0.0 all-gather.2.cloned.1.call-start
  7.2 0.7 all-gather.2.cloned.1.call-update
  7.9 1.8 reshape.127
  9.8 0.8 copy.119
  10.6 6.3 %all-to-all-start.4 = ((bf16[2,2,128,4,4]{2,4,1,0,3:T(4,128)(2,1)}), bf16[2,2,128,4,4]{2,4,1,0,3:T(4,128)(2,1)S(1)}, u32[]{:S(2)}, u32[]{:S(2)}) async-start(bf16[2,2,128,4,4]{2,4,1,0,3:T(4,128)(2,1)} %copy.119), calls=%async_computation.4 | async-start | bytes 32768 | tf_op jit(solution)/shard_map/all_to_all | solution.py:82
  16.9 0.7 broadcast_compare_fusion
  17.7 1.2 copy.121
  18.9 1.0 copy.122
  19.9 2.6 %all-to-all-done.4 = bf16[2,2,128,4,4]{2,4,1,0,3:T(4,128)(2,1)S(1)} async-done(((bf16[2,2,128,4,4]{2,4,1,0,3:T(4,128)(2,1)}), bf16[2,2,128,4,4]{2,4,1,0,3:T(4,128)(2,1)S(1)}, u32[]{:S(2)}, u32[]{:S(2)}) %all-to-all-start.4) | async-done | bytes 16416 | tf_op jit(solution)/shard_map/all_to_all | solution.py:82
  22.5 3.4 %all-to-all-start.5 = ((bf16[2,2,128,4,64]{2,4,1,0,3:T(8,128)(2,1)}), bf16[2,2,128,4,64]{2,4,1,0,3:T(8,128)(2,1)S(1)}, u32[]{:S(2)}, u32[]{:S(2)}) async-start(bf16[2,2,128,4,64]{2,4,1,0,3:T(8,128)(2,1)} %copy.122), calls=%async_computation.5 | async-start | bytes 524288 | tf_op jit(solution)/shard_map/all_to_all | solution.py:83
  26.0 31.6 %all_gather.7 = bf16[2,2,4,128,64]{4,3,2,1,0:T(8,128)(2,1)S(1)} all-gather(bf16[2,2,4,32,64]{4,3,2,1,0:T(8,128)(2,1)} %param.13), channel_id=1, replica_groups=mesh['group'=2,'seq'=4,'req'=2,'sub'=2] {'seq'}, dimensions={3}, use_global_device_ids=true | all-gather | bytes 327680 | tf_op jit(solution)/shard_map/all_gather | solution.py:72
  57.6 0.0 copy-done.4
  57.6 0.3 copy.107
  57.8 3.9 %mul.38 = f32[2,2,512,4,128]{4,3,2,1,0:T(4,128)} broadcast(f32[2,2,512,4]{3,2,1,0:T(8,128)S(1)} %copy.107), dimensions={0,1,2,3} | broadcast | bytes 4227072 | tf_op jit(solution)/shard_map/mul | solution.py:16
  61.7 0.0 copy-start.2
  61.7 5.6 %mul.39 = f32[2,2,512,512]{3,2,1,0:T(8,128)} reshape(f32[2,2,512,4,128]{4,3,2,1,0:T(4,128)} %mul.38) | data formatting | bytes 8388608 | tf_op jit(solution)/shard_map/mul | solution.py:16
  67.3 0.0 copy-done.2
  67.3 0.0 copy-start.5
  67.3 2.2 %copy.116 = bf16[2,2,512,512]{3,1,2,0:T(2,128)(2,1)S(1)} copy(bf16[2,2,512,512]{3,2,1,0:T(8,128)(2,1)S(1)} %copy-done.2) | data formatting | bytes 4194304 | tf_op args[0]
  69.5 0.0 copy-start.3
  69.5 2.0 copy.117
  71.5 0.0 copy-done.5
  71.5 0.2 fusion.17
  71.7 0.0 all-to-all-done.5
  71.7 4.5 %all-to-all-start.3 = ((bf16[2,2,128,4,512]{4,2,1,0,3:T(8,128)(2,1)}), bf16[2,2,128,4,512]{4,2,1,0,3:T(8,128)(2,1)}, u32[]{:S(2)}, u32[]{:S(2)}) async-start(bf16[2,2,128,4,512]{4,2,1,0,3:T(8,128)(2,1)} %copy.117), calls=%async_computation.3 | async-start | bytes 4194304 | tf_op jit(solution)/shard_map/all_to_all | solution.py:81
  76.3 0.0 copy-done.3
  76.3 2.7 %fusion.16 = f32[2,2,512,512]{2,3,1,0:T(8,128)} fusion(bf16[2,2,512,64]{3,2,1,0:T(8,128)(2,1)S(1)} %bitcast.80, bf16[2,2,512,64]{2,3,1,0:T(8,128)(2,1)S(1)} %copy-done.3), kind=kOutput, calls=%fused_computation.44 | convolution fusion | flops 134217728 | bytes 4718592 | tf_op jit(solution)/shard_map/vmap(vmap())/dot_general | solution.py:28
  79.0 0.0 all-gather.2.cloned.1.call-done
  79.0 0.0 copy-done
  79.0 2.3 %fusion.15 = (bf16[2,2,512]{2,1,0:T(2,128)(2,1)S(1)}, f32[2,2,512,4]{2,3,1,0:T(4,128)S(1)}) fusion(f32[2,2,512,4]{2,3,1,0:T(4,128)S(1)} %fusion.17, bf16[2,2,512,512]{3,2,1,0:T(8,128)(2,1)} %bitcast.77, bf16[2,2,4,512]{3,2,1,0:T(4,128)(2,1)S(1)} %copy-done, pred[512,4]{0,1:T(4,128)(4,1)S(1)} %fusion.8), kind=kOutput, calls=%fused_computation.43 | convolution fusion | flops 8419328 | bytes 2185216 | tf_op jit(solution)/shard_map/vmap(vmap())/dot_general | solution.py:30
  81.3 7.5 %fusion.14 = (bf16[2,2,512]{2,1,0:T(2,128)(2,1)S(1)}, f32[2,2,512,512]{2,3,1,0:T(8,128)}) fusion(f32[2,2,512,512]{2,3,1,0:T(8,128)} %fusion.16, bf16[2,2,512,512]{3,2,1,0:T(8,128)(2,1)} %bitcast.78, f32[2,2,512,512]{3,2,1,0:T(8,128)} %mul.39, bf16[2,2,512,512]{3,2,1,0:T(8,128)(2,1)S(1)} %copy-done.2, pred[2,512]{1,0:T(4,128)(4,1)S(1)} %broadcast_compare_fusion), kind=kOutput, calls=%fused_computation.42 | convolution fusion | flops 1081079808 | bytes 16782336 | tf_op jit(solution)/shard_map/vmap(vmap())/dot_general | solution.py:26
  88.8 0.1 slice_bitcast_fusion.3
  88.9 0.7 reshape.136
  89.6 0.0 copy-start.1
  89.7 3.1 %convert_reduce_fusion = f32[2,2,512]{2,1,0:T(2,128)S(1)} fusion(f32[2,2,512,512]{2,3,1,0:T(8,128)} %get-tuple-element.37, f32[2,2,512]{2,1,0:T(2,128)S(1)} %get-tuple-element.28, pred[2,512]{1,0:T(4,128)(4,1)S(1)} %broadcast_compare_fusion), kind=kLoop, calls=%fused_computation.5 | loop fusion | flops 5240832 | bytes 4211712 | tf_op jit(solution)/shard_map/vmap(vmap())/reduce_sum | solution.py:42
  92.7 0.3 copy-done.1
  93.1 5.9 %fusion.5 = f32[2,2,512,512]{3,2,1,0:T(8,128)} fusion(f32[2,2,512,512]{2,3,1,0:T(8,128)} %get-tuple-element.37, f32[2,2,512]{2,1,0:T(2,128)S(1)} %get-tuple-element.28, pred[2,512]{1,0:T(4,128)(4,1)S(1)} %broadcast_compare_fusion, f32[2,2,512,512]{3,2,1,0:T(8,128)S(1)} %copy-done.1, bf16[2,2,512,512]{3,2,1,0:T(8,128)(2,1)S(1)} %copy-done.2), kind=kOutput, calls=%fused_computation.13 | convolution fusion | flops 1080033280 | bytes 14689280 | tf_op jit(solution)/shard_map/vmap(vmap())/dot_general | solution.py:45
  99.0 22.8 %all-to-all-done.3 = bf16[2,2,128,4,512]{4,2,1,0,3:T(8,128)(2,1)} async-done(((bf16[2,2,128,4,512]{4,2,1,0,3:T(8,128)(2,1)}), bf16[2,2,128,4,512]{4,2,1,0,3:T(8,128)(2,1)}, u32[]{:S(2)}, u32[]{:S(2)}) %all-to-all-start.3) | async-done | bytes 2097184 | tf_op jit(solution)/shard_map/all_to_all | solution.py:81
  121.8 3.8 %all-to-all-start = ((bf16[4,2,256]{2,1,0:T(2,128)(2,1)}), bf16[4,2,256]{2,1,0:T(2,128)(2,1)S(1)}, u32[]{:S(2)}, u32[]{:S(2)}) async-start(bf16[4,2,256]{2,1,0:T(2,128)(2,1)} %reshape.136), calls=%async_computation | async-start | bytes 8192 | tf_op jit(solution)/shard_map/all_to_all | solution.py:99
  125.7 0.2 copy.112
  125.8 0.8 reshape.134
  126.6 4.6 %all-to-all-done = bf16[4,2,256]{2,1,0:T(2,128)(2,1)S(1)} async-done(((bf16[4,2,256]{2,1,0:T(2,128)(2,1)}), bf16[4,2,256]{2,1,0:T(2,128)(2,1)S(1)}, u32[]{:S(2)}, u32[]{:S(2)}) %all-to-all-start) | async-done | bytes 4128 | tf_op jit(solution)/shard_map/all_to_all | solution.py:99
  131.2 3.4 %all-to-all-start.2 = ((bf16[4,2,256]{2,1,0:T(2,128)(2,1)}), bf16[4,2,256]{2,1,0:T(2,128)(2,1)S(1)}, u32[]{:S(2)}, u32[]{:S(2)}) async-start(bf16[4,2,256]{2,1,0:T(2,128)(2,1)} %reshape.134), calls=%async_computation.2 | async-start | bytes 8192 | tf_op jit(solution)/shard_map/all_to_all | solution.py:107
  134.6 3.0 %add_convert_fusion = bf16[2,2,512,512]{3,2,1,0:T(8,128)(2,1)S(1)} fusion(f32[2,2,512,512]{3,2,1,0:T(8,128)} %fusion.5, bf16[2,2,4,512]{3,2,1,0:T(4,128)(2,1)S(1)} %copy-done, f32[2,2,512,4]{2,3,1,0:T(4,128)S(1)} %get-tuple-element.39, f32[2,2,512]{2,1,0:T(2,128)S(1)} %get-tuple-element.28, pred[512,4]{0,1:T(4,128)(4,1)S(1)} %fusion.8), kind=kOutput, calls=%fused_computation.6 | convolution fusion | flops 10510336 | bytes 6350848 | tf_op jit(solution)/shard_map/vmap(vmap())/dot_general | solution.py:46
  137.6 3.0 %copy.111 = bf16[1,2,2,4,128,512]{5,3,2,1,0,4:T(4,128)(2,1)} copy(bf16[1,2,2,4,128,512]{5,4,3,2,1,0:T(8,128)(2,1)S(1)} %bitcast.75) | data formatting | bytes 4194304 | tf_op jit(solution)/shard_map/broadcast_in_dim;vmap(vmap())/reshape | solution.py:97
  140.6 0.0 all-to-all-done.2
  140.6 4.9 %all-to-all-start.1 = ((bf16[1,2,2,4,128,512]{5,3,2,1,0,4:T(4,128)(2,1)}), bf16[1,2,2,4,128,512]{5,3,2,1,0,4:T(4,128)(2,1)S(1)}, u32[]{:S(2)}, u32[]{:S(2)}) async-start(bf16[1,2,2,4,128,512]{5,3,2,1,0,4:T(4,128)(2,1)} %copy.111), calls=%async_computation.1 | async-start | bytes 4194304 | tf_op jit(solution)/shard_map/all_to_all | solution.py:97
  145.4 0.6 copy_bitcast_fusion
  146.1 0.7 bitcast_bitcast_fusion
  146.8 3.1 %copy.118 = bf16[2,2,128,4,512]{4,2,3,1,0:T(8,128)(2,1)} copy(bf16[2,2,128,4,512]{4,2,1,0,3:T(8,128)(2,1)} %all-to-all-done.3) | data formatting | bytes 4194304 | tf_op jit(solution)/shard_map/all_to_all | solution.py:81
  149.9 0.1 reshape.137
  150.0 0.3 reshape.135
  150.3 0.1 copy.113
  150.4 0.1 reshape.133
  150.5 0.2 copy.109
  150.8 0.1 copy.115
  150.9 39.9 %all-to-all-done.1 = bf16[1,2,2,4,128,512]{5,3,2,1,0,4:T(4,128)(2,1)S(1)} async-done(((bf16[1,2,2,4,128,512]{5,3,2,1,0,4:T(4,128)(2,1)}), bf16[1,2,2,4,128,512]{5,3,2,1,0,4:T(4,128)(2,1)S(1)}, u32[]{:S(2)}, u32[]{:S(2)}) %all-to-all-start.1) | async-done | bytes 2097184 | tf_op jit(solution)/shard_map/all_to_all | solution.py:97
  190.8 1.5 fusion
  192.4 0.3 divide_convert_fusion
  192.6 1.1 copy.124
  (12 shorter events, 0.2 us)
Async XLA Ops:
  7.2 71.8 %copy-start = (bf16[2,2,4,512]{3,2,1,0:T(4,128)(2,1)S(1)}, bf16[2,2,4,512]{3,2,1,0:T(4,128)(2,1)}, u32[]{:S(2)}) copy-start(bf16[2,2,4,512]{3,2,1,0:T(4,128)(2,1)} %param.14) | copy-start | bytes 49156
  7.2 50.4 %copy-start.4 = (bf16[2,2,512,4]{2,3,1,0:T(4,128)(2,1)S(1)}, bf16[2,2,512,4]{2,3,1,0:T(4,128)(2,1)}, u32[]{:S(2)}) copy-start(bf16[2,2,512,4]{2,3,1,0:T(4,128)(2,1)} %param.9) | copy-start | bytes 49156
  7.2 71.8 %all-gather.2.cloned.1.call-start = ((), (), s32[]{:S(2)}) async-start(), calls=%async_computation.6 | async-start | bytes 2621440 | tf_op jit(solution)/shard_map/all_gather | solution.py:71
  10.6 11.9 %all-to-all-start.4 = ((bf16[2,2,128,4,4]{2,4,1,0,3:T(4,128)(2,1)}), bf16[2,2,128,4,4]{2,4,1,0,3:T(4,128)(2,1)S(1)}, u32[]{:S(2)}, u32[]{:S(2)}) async-start(bf16[2,2,128,4,4]{2,4,1,0,3:T(4,128)(2,1)} %copy.119), calls=%async_computation.4 | async-start | bytes 32768 | tf_op jit(solution)/shard_map/all_to_all | solution.py:82
  22.5 49.2 %all-to-all-start.5 = ((bf16[2,2,128,4,64]{2,4,1,0,3:T(8,128)(2,1)}), bf16[2,2,128,4,64]{2,4,1,0,3:T(8,128)(2,1)S(1)}, u32[]{:S(2)}, u32[]{:S(2)}) async-start(bf16[2,2,128,4,64]{2,4,1,0,3:T(8,128)(2,1)} %copy.122), calls=%async_computation.5 | async-start | bytes 524288 | tf_op jit(solution)/shard_map/all_to_all | solution.py:83
  61.7 5.6 %copy-start.2 = (bf16[2,2,512,512]{3,2,1,0:T(8,128)(2,1)S(1)}, bf16[2,2,512,512]{3,2,1,0:T(8,128)(2,1)}, u32[]{:S(2)}) copy-start(bf16[2,2,512,512]{3,2,1,0:T(8,128)(2,1)} %param.8) | copy-start | bytes 6291460
  67.3 4.2 %copy-start.5 = (bf16[2,2,4,64]{3,2,1,0:T(4,128)(2,1)S(1)}, bf16[2,2,4,64]{3,2,1,0:T(4,128)(2,1)}, u32[]{:S(2)}) copy-start(bf16[2,2,4,64]{3,2,1,0:T(4,128)(2,1)} %param.15) | copy-start | bytes 6148
  69.5 6.8 %copy-start.3 = (bf16[2,2,512,64]{2,3,1,0:T(8,128)(2,1)S(1)}, bf16[2,2,512,64]{2,3,1,0:T(8,128)(2,1)}, u32[]{:S(2)}) copy-start(bf16[2,2,512,64]{2,3,1,0:T(8,128)(2,1)} %param.10) | copy-start | bytes 786436
  71.7 50.1 %all-to-all-start.3 = ((bf16[2,2,128,4,512]{4,2,1,0,3:T(8,128)(2,1)}), bf16[2,2,128,4,512]{4,2,1,0,3:T(8,128)(2,1)}, u32[]{:S(2)}, u32[]{:S(2)}) async-start(bf16[2,2,128,4,512]{4,2,1,0,3:T(8,128)(2,1)} %copy.117), calls=%async_computation.3 | async-start | bytes 4194304 | tf_op jit(solution)/shard_map/all_to_all | solution.py:81
  89.6 3.4 %copy-start.1 = (f32[2,2,512,512]{3,2,1,0:T(8,128)S(1)}, f32[2,2,512,512]{3,2,1,0:T(8,128)}, u32[]{:S(2)}) copy-start(f32[2,2,512,512]{3,2,1,0:T(8,128)} %mul.39) | copy-start | bytes 12582916
  121.8 9.4 %all-to-all-start = ((bf16[4,2,256]{2,1,0:T(2,128)(2,1)}), bf16[4,2,256]{2,1,0:T(2,128)(2,1)S(1)}, u32[]{:S(2)}, u32[]{:S(2)}) async-start(bf16[4,2,256]{2,1,0:T(2,128)(2,1)} %reshape.136), calls=%async_computation | async-start | bytes 8192 | tf_op jit(solution)/shard_map/all_to_all | solution.py:99
  131.2 9.4 %all-to-all-start.2 = ((bf16[4,2,256]{2,1,0:T(2,128)(2,1)}), bf16[4,2,256]{2,1,0:T(2,128)(2,1)S(1)}, u32[]{:S(2)}, u32[]{:S(2)}) async-start(bf16[4,2,256]{2,1,0:T(2,128)(2,1)} %reshape.134), calls=%async_computation.2 | async-start | bytes 8192 | tf_op jit(solution)/shard_map/all_to_all | solution.py:107
  140.6 50.2 %all-to-all-start.1 = ((bf16[1,2,2,4,128,512]{5,3,2,1,0,4:T(4,128)(2,1)}), bf16[1,2,2,4,128,512]{5,3,2,1,0,4:T(4,128)(2,1)S(1)}, u32[]{:S(2)}, u32[]{:S(2)}) async-start(bf16[1,2,2,4,128,512]{5,3,2,1,0,4:T(4,128)(2,1)} %copy.111), calls=%async_computation.1 | async-start | bytes 4194304 | tf_op jit(solution)/shard_map/all_to_all | solution.py:97
Sparse Core Ops, SparseCore 0:
  9.6 62.4 all-gather.1
